TPU v7x, 32 devices: a whole 2x2x4 slice. The times are simulated.
32 devices in a mesh: gx: 8 (over y, x, core), gy: 4 (over z).
Axes of the slice: x: 2, y: 2, z: 4, core: 2. Of those that a mesh axis runs over, the one named last changes fastest.
Arguments:
- tiles: float32 [256, 5, 128, 128], P(('gx', 'gy')), may hold values from 0 to 0.003125
- cols: int32 [256, 5], P(('gx', 'gy')), may hold values from 0 to 17, as said below
- boundary: int32 [32, 2], P(('gx', 'gy')), may hold values from 0 to 7, as said below
- current: float32 [32768, 64], P(('gx', 'gy')), may hold values from -44 to 44
- previous: float32 [32768, 64], P(('gx', 'gy')), may hold values from -44 to 44
Outputs:
- filtered: float32 [32768, 64], P(('gx', 'gy'))
- gram: float32 [64, 64], replicated
Inputs may be any that keep to these rules, and one draw needn't show every extreme that they name: `cols`: in each part, block row r has r in its first tile slot; each value from 8 up to the table's last entry occurs exactly once among the part's block rows. `boundary`: the 2 entries of a row are distinct block rows of the part.
All inputs are finite; a program needn't handle non-finite values.
Results may differ from a plain program's by a relative error of at most 0.0003.
Values sent between devices are 32-bit elements; how exact they have to be, the bound alone decides.
A program may use at most 64 MiB of HBM per device.

v0:
```python
import jax
import jax.numpy as jnp
from jax import lax
from jax.sharding import PartitionSpec as P

ITERS = 3


def partner(value, axis, stride):
    mask = 2**stride
    pairs = [(source, source ^ mask) for source in range(lax.axis_size(axis))]
    return lax.ppermute(value, axis, pairs)


def shards(tiles, cols, boundary, current, previous):
    size_x = lax.axis_size("gx")
    size_y = lax.axis_size("gy")
    block_rows = cols.shape[0]
    block_size = tiles.shape[-1]
    vectors = current.shape[1]
    bits_low = list(range(size_y.bit_length() - 1))
    bits_high = list(range(size_x.bit_length() - 1))
    field = current
    older = previous
    for step in range(ITERS):
        blocks = field.reshape(block_rows, block_size, vectors)
        outgoing = jnp.take(blocks, boundary[0], axis=0)

        def from_low():
            return [partner(outgoing, "gy", which_bit) for which_bit in bits_low]

        def from_high():
            return [partner(outgoing, "gx", which_bit) for which_bit in bits_high]

        low_ghosts = from_low()
        high_ghosts = from_high()
        table = jnp.concatenate([blocks] + low_ghosts + high_ghosts, axis=0)
        operands = jnp.take(table, cols, axis=0)
        product = jnp.einsum("rtij,rtjv->riv", tiles, operands, precision=lax.Precision.HIGHEST)
        product = product.reshape(block_rows * block_size, vectors)
        nexter = 2.0 / 0.75 * (product - 0.25 * field) - older
        older = field
        field = nexter
    partial_gram = jnp.dot(
        field.T, field, precision=lax.Precision.HIGHEST, preferred_element_type=jnp.float32
    )
    total_rows = block_rows * block_size * size_x * size_y
    gram = lax.psum(partial_gram, ("gx", "gy")) / float(total_rows)
    return (field, gram)


def solution(mesh):
    in_specs = (
        P(("gx", "gy"), None, None, None),
        P(("gx", "gy"), None),
        P(("gx", "gy"), None),
        P(("gx", "gy"), None),
        P(("gx", "gy"), None),
    )
    out_specs = (P(("gx", "gy"), None), P())
    return jax.shard_map(shards, mesh=mesh, in_specs=in_specs, out_specs=out_specs, check_vma=False)
```

profile of v0, /device:TPU:0, one launch (start us, length us, event | category | flops | bytes accessed | tf_op | source)
XLA Modules:
  0.0 96.7 jit_solution(13172485153724881354)
XLA Ops:
  0.6 0.0 copy-start
  0.6 0.8 compare_and_fusion.1
  1.5 0.7 compare_select_fusion.1
  2.1 1.0 copy_bitcast_fusion.2
  3.1 0.6 gather_fusion
  3.7 0.1 broadcast_select_fusion.2
  3.7 3.0 %collective-permute-start.4 = (f32[2,128,64]{1,2,0:T(8,128)S(1)}, f32[2,128,64]{1,2,0:T(8,128)S(1)}, u32[]{:S(2)}, u32[]{:S(2)}) collective-permute-start(f32[2,128,64]{1,2,0:T(8,128)S(1)} %broadcast_select_fusion.2), channel_id=1, source_target_pairs={{0,16},{4,20},{8,24},{12,28},{16,0},{20,4},{24,8},{28,12},{1,17},{... | collective-permute-start | bytes 196616 | tf_op jit(solution)/shard_map/ppermute | solution.py:12
  6.7 1.5 %collective-permute-start.3 = (f32[2,128,64]{1,2,0:T(8,128)S(1)}, f32[2,128,64]{1,2,0:T(8,128)S(1)}, u32[]{:S(2)}, u32[]{:S(2)}) collective-permute-start(f32[2,128,64]{1,2,0:T(8,128)S(1)} %broadcast_select_fusion.2), channel_id=1, source_target_pairs={{0,8},{4,12},{8,0},{12,4},{16,24},{20,28},{24,16},{28,20},{1,9},{5... | collective-permute-start | bytes 196616 | tf_op jit(solution)/shard_map/ppermute | solution.py:12
  8.2 0.0 collective-permute-start.2
  8.2 2.6 %collective-permute-start.1 = (f32[2,128,64]{1,2,0:T(8,128)S(1)}, f32[2,128,64]{1,2,0:T(8,128)S(1)}, u32[]{:S(2)}, u32[]{:S(2)}) collective-permute-start(f32[2,128,64]{1,2,0:T(8,128)S(1)} %broadcast_select_fusion.2), channel_id=1, source_target_pairs={{0,2},{1,3},{2,0},{3,1},{4,6},{5,7},{6,4},{7,5},{8,10},{9,11},{10,... | collective-permute-start | bytes 196616 | tf_op jit(solution)/shard_map/ppermute | solution.py:12
  10.8 1.6 %collective-permute-start = (f32[2,128,64]{1,2,0:T(8,128)S(1)}, f32[2,128,64]{1,2,0:T(8,128)}, u32[]{:S(2)}, u32[]{:S(2)}) collective-permute-start(f32[2,128,64]{1,2,0:T(8,128)S(1)} %broadcast_select_fusion.2), channel_id=1, source_target_pairs={{0,1},{1,0},{2,3},{3,2},{4,5},{5,4},{6,7},{7,6},{8,9},{9,8},{10,11... | collective-permute-start | bytes 196616 | tf_op jit(solution)/shard_map/ppermute | solution.py:12
  12.4 0.7 compare_and_fusion
  13.1 0.7 compare_select_fusion
  13.8 1.0 constant_dynamic-update-slice_fusion.5
  14.7 0.6 reshape.97
  15.3 0.7 pad_clamp_fusion
  16.0 0.0 collective-permute-done
  16.0 0.8 constant_dynamic-update-slice_fusion.4
  16.8 0.0 collective-permute-done.1
  16.8 0.0 collective-permute-done.2
  16.9 0.0 collective-permute-done.3
  16.9 0.0 collective-permute-done.4
  16.9 1.7 %gather_fusion.1 = f32[40,128,64]{1,2,0:T(8,128)} fusion(f32[18,128,64]{1,2,0:T(8,128)S(1)} %constant_dynamic-update-slice_fusion, s32[1024]{0:T(1024)S(1)} %pad_clamp_fusion), kind=kCustom, calls=%fused_computation.1.clone | custom fusion | bytes 2621600 | tf_op jit(solution)/shard_map/jit(_take)/gather | solution.py:38
  18.6 4.7 %fusion.6 = f32[8,8,8,128]{3,2,1,0:T(8,128)S(1)} fusion(f32[8,5,128,128]{3,2,1,0:T(8,128)S(1)} %copy-done, f32[8,5,128,64]{2,3,1,0:T(8,128)} %bitcast.85, pred[8,5]{1,0:T(8,128)(4,1)S(1)} %compare_and_fusion), kind=kOutput, calls=%fused_computation.12 | convolution fusion | flops 503644160 | bytes 4194344 | tf_op jit(solution)/shard_map/rtij,rtjv->riv/dot_general | solution.py:39
  23.4 0.0 copy-start.2
  23.4 0.7 copy-done.2
  24.1 0.1 copy_bitcast_fusion.1
  24.1 0.6 gather_fusion.2
  24.7 0.1 broadcast_select_fusion.1
  24.8 0.5 collective-permute-start.9
  25.3 0.5 collective-permute-start.8
  25.8 0.0 collective-permute-start.7
  25.8 0.8 collective-permute-start.6
  26.6 1.5 %collective-permute-start.5 = (f32[2,128,64]{1,2,0:T(8,128)S(1)}, f32[2,128,64]{1,2,0:T(8,128)S(1)}, u32[]{:S(2)}, u32[]{:S(2)}) collective-permute-start(f32[2,128,64]{1,2,0:T(8,128)S(1)} %broadcast_select_fusion.1), channel_id=1, source_target_pairs={{0,1},{1,0},{2,3},{3,2},{4,5},{5,4},{6,7},{7,6},{8,9},{9,8},{10,11... | collective-permute-start | bytes 196616 | tf_op jit(solution)/shard_map/ppermute | solution.py:12
  28.1 1.1 %constant_dynamic-update-slice_fusion.11 = f32[18,128,64]{1,2,0:T(8,128)S(1)} fusion(f32[1024,64]{0,1:T(8,128)} %param.13, f32[1024,64]{0,1:T(8,128)S(1)} %copy-done.1, f32[8,8,8,128]{3,2,1,0:T(8,128)} %copy-done.2), kind=kLoop, calls=%fused_computation.45 | loop fusion | flops 262143 | bytes 1048576
  29.1 2.0 %collective-permute-done.5 = f32[2,128,64]{1,2,0:T(8,128)S(1)} collective-permute-done((f32[2,128,64]{1,2,0:T(8,128)S(1)}, f32[2,128,64]{1,2,0:T(8,128)S(1)}, u32[]{:S(2)}, u32[]{:S(2)}) %collective-permute-start.5) | collective-permute-done | bytes 65568 | tf_op jit(solution)/shard_map/ppermute | solution.py:12
  31.2 1.4 %collective-permute-done.6 = f32[2,128,64]{1,2,0:T(8,128)S(1)} collective-permute-done((f32[2,128,64]{1,2,0:T(8,128)S(1)}, f32[2,128,64]{1,2,0:T(8,128)S(1)}, u32[]{:S(2)}, u32[]{:S(2)}) %collective-permute-start.6) | collective-permute-done | bytes 65568 | tf_op jit(solution)/shard_map/ppermute | solution.py:12
  32.7 0.0 collective-permute-done.7
  32.7 0.0 collective-permute-done.8
  32.7 0.0 collective-permute-done.9
  32.7 1.7 %gather_fusion.3 = f32[40,128,64]{1,2,0:T(8,128)} fusion(f32[18,128,64]{1,2,0:T(8,128)S(1)} %constant_dynamic-update-slice_fusion.6, s32[1024]{0:T(1024)S(1)} %pad_clamp_fusion), kind=kCustom, calls=%fused_computation.4.clone | custom fusion | bytes 2621600 | tf_op jit(solution)/shard_map/jit(_take)/gather | solution.py:38
  34.4 4.8 %fusion.9 = f32[8,8,8,128]{3,2,1,0:T(8,128)S(1)} fusion(f32[8,5,128,128]{3,2,1,0:T(8,128)S(1)} %copy-done, f32[8,5,128,64]{2,3,1,0:T(8,128)} %bitcast.86, pred[8,5]{1,0:T(8,128)(4,1)S(1)} %compare_and_fusion), kind=kOutput, calls=%fused_computation.13 | convolution fusion | flops 503644160 | bytes 4194344 | tf_op jit(solution)/shard_map/rtij,rtjv->riv/dot_general | solution.py:39
  39.2 0.1 fusion.27
  39.3 0.6 copy-done.8
  39.9 0.7 copy-done.10
  40.6 0.6 gather_fusion.4
  41.2 0.1 broadcast_select_fusion
  41.2 1.5 %collective-permute-start.14 = (f32[2,128,64]{1,2,0:T(8,128)S(1)}, f32[2,128,64]{1,2,0:T(8,128)S(1)}, u32[]{:S(2)}, u32[]{:S(2)}) collective-permute-start(f32[2,128,64]{1,2,0:T(8,128)S(1)} %broadcast_select_fusion), channel_id=1, source_target_pairs={{0,16},{4,20},{8,24},{12,28},{16,0},{20,4},{24,8},{28,12},{1,17},{... | collective-permute-start | bytes 196616 | tf_op jit(solution)/shard_map/ppermute | solution.py:12
  42.8 1.5 %collective-permute-start.13 = (f32[2,128,64]{1,2,0:T(8,128)S(1)}, f32[2,128,64]{1,2,0:T(8,128)S(1)}, u32[]{:S(2)}, u32[]{:S(2)}) collective-permute-start(f32[2,128,64]{1,2,0:T(8,128)S(1)} %broadcast_select_fusion), channel_id=1, source_target_pairs={{0,8},{4,12},{8,0},{12,4},{16,24},{20,28},{24,16},{28,20},{1,9},{5... | collective-permute-start | bytes 196616 | tf_op jit(solution)/shard_map/ppermute | solution.py:12
  44.3 0.0 collective-permute-start.12
  44.3 0.9 collective-permute-start.11
  45.2 1.7 %collective-permute-start.10 = (f32[2,128,64]{1,2,0:T(8,128)S(1)}, f32[2,128,64]{1,2,0:T(8,128)S(1)}, u32[]{:S(2)}, u32[]{:S(2)}) collective-permute-start(f32[2,128,64]{1,2,0:T(8,128)S(1)} %broadcast_select_fusion), channel_id=1, source_target_pairs={{0,1},{1,0},{2,3},{3,2},{4,5},{5,4},{6,7},{7,6},{8,9},{9,8},{10,11... | collective-permute-start | bytes 196616 | tf_op jit(solution)/shard_map/ppermute | solution.py:12
  46.8 1.0 constant_dynamic-update-slice_fusion.17
  47.8 3.0 %collective-permute-done.10 = f32[2,128,64]{1,2,0:T(8,128)S(1)} collective-permute-done((f32[2,128,64]{1,2,0:T(8,128)S(1)}, f32[2,128,64]{1,2,0:T(8,128)S(1)}, u32[]{:S(2)}, u32[]{:S(2)}) %collective-permute-start.10) | collective-permute-done | bytes 65568 | tf_op jit(solution)/shard_map/ppermute | solution.py:12
  50.8 0.0 collective-permute-done.11
  50.8 0.0 collective-permute-done.12
  50.9 0.0 collective-permute-done.14
  50.9 1.7 %gather_fusion.5 = f32[40,128,64]{1,2,0:T(8,128)} fusion(f32[18,128,64]{1,2,0:T(8,128)S(1)} %constant_dynamic-update-slice_fusion.12, s32[1024]{0:T(1024)S(1)} %pad_clamp_fusion), kind=kCustom, calls=%fused_computation.5.clone | custom fusion | bytes 2621600 | tf_op jit(solution)/shard_map/jit(_take)/gather | solution.py:38
  52.6 4.8 %fusion.12 = f32[8,8,8,128]{3,2,1,0:T(8,128)S(1)} fusion(f32[8,5,128,128]{3,2,1,0:T(8,128)S(1)} %copy-done, f32[8,5,128,64]{2,3,1,0:T(8,128)} %bitcast.84, pred[8,5]{1,0:T(8,128)(4,1)S(1)} %compare_and_fusion), kind=kOutput, calls=%fused_computation.14 | convolution fusion | flops 503644160 | bytes 4194344 | tf_op jit(solution)/shard_map/rtij,rtjv->riv/dot_general | solution.py:39
  57.4 0.1 fusion.22
  57.5 0.0 copy-start.11
  57.5 0.4 fusion.32
  57.9 38.2 %psum.7 = f32[64,64]{1,0:T(8,128)S(1)} all-reduce(f32[64,64]{1,0:T(8,128)S(1)} %fusion.32), channel_id=1, replica_groups=mesh['gx'=8,'gy'=4] {'gx','gy'}, use_global_device_ids=true, to_apply=%region_0.3 | all-reduce | flops 4096 | bytes 32768 | tf_op jit(solution)/shard_map/psum | solution.py:48
  96.1 0.6 broadcast_multiply_fusion
  (35 shorter events, 0.2 us)
Async XLA Ops:
  0.6 18.0 %copy-start = (f32[8,5,128,128]{3,2,1,0:T(8,128)S(1)}, f32[8,5,128,128]{3,2,1,0:T(8,128)}, u32[]{:S(2)}) copy-start(f32[8,5,128,128]{3,2,1,0:T(8,128)} %param.9) | copy-start | bytes 7864324
  3.7 13.2 %collective-permute-start.4 = (f32[2,128,64]{1,2,0:T(8,128)S(1)}, f32[2,128,64]{1,2,0:T(8,128)S(1)}, u32[]{:S(2)}, u32[]{:S(2)}) collective-permute-start(f32[2,128,64]{1,2,0:T(8,128)S(1)} %broadcast_select_fusion.2), channel_id=1, source_target_pairs={{0,16},{4,20},{8,24},{12,28},{16,0},{20,4},{24,8},{28,12},{1,17},{... | collective-permute-start | bytes 196616 | tf_op jit(solution)/shard_map/ppermute | solution.py:12
  6.7 10.2 %collective-permute-start.3 = (f32[2,128,64]{1,2,0:T(8,128)S(1)}, f32[2,128,64]{1,2,0:T(8,128)S(1)}, u32[]{:S(2)}, u32[]{:S(2)}) collective-permute-start(f32[2,128,64]{1,2,0:T(8,128)S(1)} %broadcast_select_fusion.2), channel_id=1, source_target_pairs={{0,8},{4,12},{8,0},{12,4},{16,24},{20,28},{24,16},{28,20},{1,9},{5... | collective-permute-start | bytes 196616 | tf_op jit(solution)/shard_map/ppermute | solution.py:12
  8.2 8.6 %collective-permute-start.2 = (f32[2,128,64]{1,2,0:T(8,128)S(1)}, f32[2,128,64]{1,2,0:T(8,128)S(1)}, u32[]{:S(2)}, u32[]{:S(2)}) collective-permute-start(f32[2,128,64]{1,2,0:T(8,128)S(1)} %broadcast_select_fusion.2), channel_id=1, source_target_pairs={{0,4},{4,0},{8,12},{12,8},{16,20},{20,16},{24,28},{28,24},{1,5},{5... | collective-permute-start | bytes 196616 | tf_op jit(solution)/shard_map/ppermute | solution.py:12
  8.2 8.6 %collective-permute-start.1 = (f32[2,128,64]{1,2,0:T(8,128)S(1)}, f32[2,128,64]{1,2,0:T(8,128)S(1)}, u32[]{:S(2)}, u32[]{:S(2)}) collective-permute-start(f32[2,128,64]{1,2,0:T(8,128)S(1)} %broadcast_select_fusion.2), channel_id=1, source_target_pairs={{0,2},{1,3},{2,0},{3,1},{4,6},{5,7},{6,4},{7,5},{8,10},{9,11},{10,... | collective-permute-start | bytes 196616 | tf_op jit(solution)/shard_map/ppermute | solution.py:12
  10.8 5.2 %collective-permute-start = (f32[2,128,64]{1,2,0:T(8,128)S(1)}, f32[2,128,64]{1,2,0:T(8,128)}, u32[]{:S(2)}, u32[]{:S(2)}) collective-permute-start(f32[2,128,64]{1,2,0:T(8,128)S(1)} %broadcast_select_fusion.2), channel_id=1, source_target_pairs={{0,1},{1,0},{2,3},{3,2},{4,5},{5,4},{6,7},{7,6},{8,9},{9,8},{10,11... | collective-permute-start | bytes 196616 | tf_op jit(solution)/shard_map/ppermute | solution.py:12
  18.6 5.5 %copy-start.1 = (f32[1024,64]{0,1:T(8,128)S(1)}, f32[1024,64]{0,1:T(8,128)}, u32[]{:S(2)}) copy-start(f32[1024,64]{0,1:T(8,128)} %param.12) | copy-start | bytes 786436
  18.6 5.5 %copy-start.5 = (f32[1024,64]{0,1:T(8,128)S(1)}, f32[1024,64]{0,1:T(8,128)}, u32[]{:S(2)}) copy-start(f32[1024,64]{0,1:T(8,128)} %param.13) | copy-start | bytes 786436
  23.4 0.7 copy-start.2
  24.8 7.9 %collective-permute-start.9 = (f32[2,128,64]{1,2,0:T(8,128)S(1)}, f32[2,128,64]{1,2,0:T(8,128)S(1)}, u32[]{:S(2)}, u32[]{:S(2)}) collective-permute-start(f32[2,128,64]{1,2,0:T(8,128)S(1)} %broadcast_select_fusion.1), channel_id=1, source_target_pairs={{0,16},{4,20},{8,24},{12,28},{16,0},{20,4},{24,8},{28,12},{1,17},{... | collective-permute-start | bytes 196616 | tf_op jit(solution)/shard_map/ppermute | solution.py:12
  25.3 7.4 %collective-permute-start.8 = (f32[2,128,64]{1,2,0:T(8,128)S(1)}, f32[2,128,64]{1,2,0:T(8,128)S(1)}, u32[]{:S(2)}, u32[]{:S(2)}) collective-permute-start(f32[2,128,64]{1,2,0:T(8,128)S(1)} %broadcast_select_fusion.1), channel_id=1, source_target_pairs={{0,8},{4,12},{8,0},{12,4},{16,24},{20,28},{24,16},{28,20},{1,9},{5... | collective-permute-start | bytes 196616 | tf_op jit(solution)/shard_map/ppermute | solution.py:12
  25.8 6.8 %collective-permute-start.7 = (f32[2,128,64]{1,2,0:T(8,128)S(1)}, f32[2,128,64]{1,2,0:T(8,128)S(1)}, u32[]{:S(2)}, u32[]{:S(2)}) collective-permute-start(f32[2,128,64]{1,2,0:T(8,128)S(1)} %broadcast_select_fusion.1), channel_id=1, source_target_pairs={{0,4},{4,0},{8,12},{12,8},{16,20},{20,16},{24,28},{28,24},{1,5},{5... | collective-permute-start | bytes 196616 | tf_op jit(solution)/shard_map/ppermute | solution.py:12
  25.8 6.8 %collective-permute-start.6 = (f32[2,128,64]{1,2,0:T(8,128)S(1)}, f32[2,128,64]{1,2,0:T(8,128)S(1)}, u32[]{:S(2)}, u32[]{:S(2)}) collective-permute-start(f32[2,128,64]{1,2,0:T(8,128)S(1)} %broadcast_select_fusion.1), channel_id=1, source_target_pairs={{0,2},{1,3},{2,0},{3,1},{4,6},{5,7},{6,4},{7,5},{8,10},{9,11},{10,... | collective-permute-start | bytes 196616 | tf_op jit(solution)/shard_map/ppermute | solution.py:12
  26.6 4.6 %collective-permute-start.5 = (f32[2,128,64]{1,2,0:T(8,128)S(1)}, f32[2,128,64]{1,2,0:T(8,128)S(1)}, u32[]{:S(2)}, u32[]{:S(2)}) collective-permute-start(f32[2,128,64]{1,2,0:T(8,128)S(1)} %broadcast_select_fusion.1), channel_id=1, source_target_pairs={{0,1},{1,0},{2,3},{3,2},{4,5},{5,4},{6,7},{7,6},{8,9},{9,8},{10,11... | collective-permute-start | bytes 196616 | tf_op jit(solution)/shard_map/ppermute | solution.py:12
  34.4 4.8 %copy-start.3 = (f32[8,8,8,128]{3,2,1,0:T(8,128)S(1)}, f32[8,8,8,128]{3,2,1,0:T(8,128)}, u32[]{:S(2)}) copy-start(f32[8,8,8,128]{3,2,1,0:T(8,128)} %copy-done.2) | copy-start | bytes 786436
  34.4 4.8 %copy-start.6 = (f32[1024,64]{0,1:T(8,128)S(1)}, f32[1024,64]{0,1:T(8,128)}, u32[]{:S(2)}) copy-start(f32[1024,64]{0,1:T(8,128)} %param.13) | copy-start | bytes 786436
  39.2 0.7 copy-start.8
  39.9 0.7 copy-start.10
  41.2 9.6 %collective-permute-start.14 = (f32[2,128,64]{1,2,0:T(8,128)S(1)}, f32[2,128,64]{1,2,0:T(8,128)S(1)}, u32[]{:S(2)}, u32[]{:S(2)}) collective-permute-start(f32[2,128,64]{1,2,0:T(8,128)S(1)} %broadcast_select_fusion), channel_id=1, source_target_pairs={{0,16},{4,20},{8,24},{12,28},{16,0},{20,4},{24,8},{28,12},{1,17},{... | collective-permute-start | bytes 196616 | tf_op jit(solution)/shard_map/ppermute | solution.py:12
  42.8 8.1 %collective-permute-start.13 = (f32[2,128,64]{1,2,0:T(8,128)S(1)}, f32[2,128,64]{1,2,0:T(8,128)S(1)}, u32[]{:S(2)}, u32[]{:S(2)}) collective-permute-start(f32[2,128,64]{1,2,0:T(8,128)S(1)} %broadcast_select_fusion), channel_id=1, source_target_pairs={{0,8},{4,12},{8,0},{12,4},{16,24},{20,28},{24,16},{28,20},{1,9},{5... | collective-permute-start | bytes 196616 | tf_op jit(solution)/shard_map/ppermute | solution.py:12
  44.3 6.6 %collective-permute-start.12 = (f32[2,128,64]{1,2,0:T(8,128)S(1)}, f32[2,128,64]{1,2,0:T(8,128)S(1)}, u32[]{:S(2)}, u32[]{:S(2)}) collective-permute-start(f32[2,128,64]{1,2,0:T(8,128)S(1)} %broadcast_select_fusion), channel_id=1, source_target_pairs={{0,4},{4,0},{8,12},{12,8},{16,20},{20,16},{24,28},{28,24},{1,5},{5... | collective-permute-start | bytes 196616 | tf_op jit(solution)/shard_map/ppermute | solution.py:12
  44.3 6.5 %collective-permute-start.11 = (f32[2,128,64]{1,2,0:T(8,128)S(1)}, f32[2,128,64]{1,2,0:T(8,128)S(1)}, u32[]{:S(2)}, u32[]{:S(2)}) collective-permute-start(f32[2,128,64]{1,2,0:T(8,128)S(1)} %broadcast_select_fusion), channel_id=1, source_target_pairs={{0,2},{1,3},{2,0},{3,1},{4,6},{5,7},{6,4},{7,5},{8,10},{9,11},{10,... | collective-permute-start | bytes 196616 | tf_op jit(solution)/shard_map/ppermute | solution.py:12
  45.2 5.6 %collective-permute-start.10 = (f32[2,128,64]{1,2,0:T(8,128)S(1)}, f32[2,128,64]{1,2,0:T(8,128)S(1)}, u32[]{:S(2)}, u32[]{:S(2)}) collective-permute-start(f32[2,128,64]{1,2,0:T(8,128)S(1)} %broadcast_select_fusion), channel_id=1, source_target_pairs={{0,1},{1,0},{2,3},{3,2},{4,5},{5,4},{6,7},{7,6},{8,9},{9,8},{10,11... | collective-permute-start | bytes 196616 | tf_op jit(solution)/shard_map/ppermute | solution.py:12
  52.6 4.8 %copy-start.4 = (f32[8,8,8,128]{3,2,1,0:T(8,128)S(1)}, f32[8,8,8,128]{3,2,1,0:T(8,128)}, u32[]{:S(2)}) copy-start(f32[8,8,8,128]{3,2,1,0:T(8,128)} %copy-done.2) | copy-start | bytes 786436
  52.6 4.8 %copy-start.7 = (f32[1024,64]{0,1:T(8,128)S(1)}, f32[1024,64]{0,1:T(8,128)}, u32[]{:S(2)}) copy-start(f32[1024,64]{0,1:T(8,128)} %param.13) | copy-start | bytes 786436
  52.6 4.8 %copy-start.9 = (f32[8,8,8,128]{3,2,1,0:T(8,128)S(1)}, f32[8,8,8,128]{3,2,1,0:T(8,128)}, u32[]{:S(2)}) copy-start(f32[8,8,8,128]{3,2,1,0:T(8,128)} %copy-done.8) | copy-start | bytes 786436
  57.5 39.2 %copy-start.11 = (f32[1024,64]{0,1:T(8,128)}, f32[1024,64]{0,1:T(8,128)S(1)}, u32[]{:S(2)}) copy-start(f32[1024,64]{0,1:T(8,128)S(1)} %fusion.22) | copy-start | bytes 786436
where the time goes:
time: 97.2 us; the launch traced here: 96.7 us
  blocking collectives  38.2 us (39%)
  starting transfers between devices  17.5 us (18%)
  matrix products  14.6 us (15%)
  local copies, waits for them, and re-layouts  13.2 us (14%)
  waiting for transfers between devices  6.51 us (7%)
  other arithmetic  5.71 us (6%)
    psum x1, blocking collectives, shards(): gram = lax.psum(partial_gram, ('gx', 'gy')) / float(total_rows)  38.2 us
    ppermute x15, starting transfers between devices, partner(): return lax.ppermute(value, axis, pairs)  17.5 us
    dot_general x3, matrix products, shards(): jnp.einsum('rtij,rtjv->riv', tiles, operands, precision=lax.Precision.HIG...  14.3 us
    ppermute x15, waiting for transfers between devices, partner(): return lax.ppermute(value, axis, pairs)  6.51 us
    gather x3, local copies, waits for them, and re-layouts, shards(): operands = jnp.take(table, cols, axis=0)  5.09 us
    unnamed x38, local copies, waits for them, and re-layouts  4.88 us
  transfers between devices with their start and end apart: 15, of which 3 were waited for; matrix products, arithmetic and copies ran while one was open for 7% of the time, Pallas kernels for 0%

commit v1 on v0

v1 whole, which is shorter than its diff:
```python
import functools

import jax
import jax.numpy as jnp
from jax import lax
from jax.experimental import pallas as pl
from jax.experimental.pallas import tpu as pltpu
from jax.sharding import PartitionSpec as P

ITERS = 3
MESH = pl.DeviceIdType.MESH


def contract(a, b):
    return lax.dot_general(a, b, (((1,), (1,)), ((), ())), preferred_element_type=jnp.float32)


def split(x):
    high = x.astype(jnp.bfloat16)
    return high, (x - high.astype(jnp.float32)).astype(jnp.bfloat16)


def kernel(
    size_x,
    size_y,
    total_rows,
    cols,
    boundary,
    tiles,
    current,
    previous,
    filtered,
    gram,
    raw,
    pairs,
    table,
    fields,
    outgoing,
    ghosts,
    terms_y,
    terms_x,
    tile_sem,
    send_sem,
    recv_sem,
    send_y,
    recv_y,
    send_x,
    recv_x,
):
    block_rows, per_row, block, _ = raw.shape
    vectors = fields.shape[2]
    shared = outgoing.shape[1]
    i = lax.axis_index("gx")
    j = lax.axis_index("gy")

    partners = []
    for axis, size, me in (("gy", size_y, j), ("gx", size_x, i)):
        for bit in range(size.bit_length() - 1):
            stride = 2**bit
            partners.append({axis: me + stride - 2 * stride * ((me // stride) % 2)})
    peers_y = [{"gy": (j + k) % size_y} for k in range(1, size_y)]
    peers_x = [{"gx": (i + k) % size_x} for k in range(1, size_x)]

    barrier = pltpu.get_barrier_semaphore()
    for peer in peers_y + peers_x:
        pl.semaphore_signal(barrier, inc=1, device_id=peer, device_id_type=MESH)

    loads = [pltpu.make_async_copy(tiles.at[r], raw.at[r], tile_sem.at[r]) for r in range(block_rows)]
    for load in loads:
        load.start()

    for r in range(block_rows):
        fields[0, r] = previous[:, r * block : (r + 1) * block]
        fields[1, r] = current[:, r * block : (r + 1) * block]
    for s in range(shared):
        outgoing[0, s] = fields[1, boundary[0, s]]

    pl.semaphore_wait(barrier, len(peers_y) + len(peers_x))

    def exchange(step):
        copies = []
        for b, partner in enumerate(partners):
            copies.append(
                pltpu.make_async_remote_copy(
                    src_ref=outgoing.at[step],
                    dst_ref=ghosts.at[step, b],
                    send_sem=send_sem.at[step, b],
                    recv_sem=recv_sem.at[step, b],
                    device_id=partner,
                    device_id_type=MESH,
                )
            )
        for copy in copies:
            copy.start()
        return copies

    def enter(entry, value):
        high, low = split(value)
        table[entry, :vectors, :] = high
        table[entry, vectors:, :] = low

    def advance(step, r):
        operand = jnp.concatenate([table[cols[r, t]] for t in range(per_row)], axis=1)
        parts = contract(operand, pairs[r])
        product = parts[:vectors, :block] + (parts[vectors:, :block] + parts[:vectors, block:])
        return 2.0 / 0.75 * (product - 0.25 * fields[step + 1, r]) - fields[step, r]

    copies = exchange(0)
    started = list(copies)
    for r in range(block_rows):
        enter(r, fields[1, r])
    for r in range(block_rows):
        loads[r].wait()
        for t in range(per_row):
            high, low = split(raw[r, t])
            pairs[r, :block, t * block : (t + 1) * block] = high
            pairs[r, block:, t * block : (t + 1) * block] = low

    for step in range(ITERS):
        for b, copy in enumerate(copies):
            copy.wait_recv()
            for s in range(shared):
                enter(block_rows + b * shared + s, ghosts[step, b, s])
        if step < ITERS - 1:
            for s in range(shared):
                outgoing[step + 1, s] = advance(step, boundary[0, s])
            copies = exchange(step + 1)
            started += copies
            for r in range(block_rows):
                fields[step + 2, r] = advance(step, r)
            for r in range(block_rows):
                enter(r, fields[step + 2, r])
        else:
            halves = []
            for r in range(block_rows):
                value = advance(step, r)
                filtered[:, r * block : (r + 1) * block] = value
                halves.append(jnp.concatenate(split(value), axis=0))
            whole = jnp.concatenate(halves, axis=1)
            parts = contract(whole, whole)
            total = parts[:vectors, :vectors] + (parts[vectors:, :vectors] + parts[:vectors, vectors:])

    half = vectors // 2

    def share(total, me, axis, peers, terms, send, recv):
        terms[me] = total
        moves = []
        for k, peer in enumerate(peers):
            moves.append(
                pltpu.make_async_remote_copy(
                    src_ref=terms.at[me],
                    dst_ref=terms.at[me],
                    send_sem=send.at[k],
                    recv_sem=recv.at[k],
                    device_id=peer,
                    device_id_type=MESH,
                )
            )
        for move in moves:
            move.start()
        for move in moves:
            move.wait_recv()
        result = terms[0]
        for k in range(1, terms.shape[0]):
            result = result + terms[k]
        return result, moves

    total = jnp.concatenate([total[:half], total[half:]], axis=1)
    total, moves = share(total, j, "gy", peers_y, terms_y, send_y, recv_y)
    started += moves
    total, moves = share(total, i, "gx", peers_x, terms_x, send_x, recv_x)
    started += moves
    total = total / float(total_rows)
    gram[:half, :] = total[:, :vectors]
    gram[half:, :] = total[:, vectors:]
    for copy in started:
        copy.wait_send()


def shards(tiles, cols, boundary, current, previous):
    size_x = lax.axis_size("gx")
    size_y = lax.axis_size("gy")
    block_rows, per_row, block, _ = tiles.shape
    rows, vectors = current.shape
    shared = boundary.shape[1]
    bits = (size_x * size_y).bit_length() - 1
    entries = block_rows + bits * shared
    vmem = pl.BlockSpec(memory_space=pltpu.VMEM)
    smem = pl.BlockSpec(memory_space=pltpu.SMEM)
    dma = pltpu.SemaphoreType.DMA
    filtered, gram = pl.pallas_call(
        functools.partial(kernel, size_x, size_y, rows * size_x * size_y),
        out_shape=(
            jax.ShapeDtypeStruct((vectors, rows), jnp.float32),
            jax.ShapeDtypeStruct((vectors, vectors), jnp.float32),
        ),
        in_specs=[smem, smem, pl.BlockSpec(memory_space=pl.ANY), vmem, vmem],
        out_specs=(vmem, vmem),
        scratch_shapes=[
            pltpu.VMEM(tiles.shape, jnp.float32),
            pltpu.VMEM((block_rows, 2 * block, per_row * block), jnp.bfloat16),
            pltpu.VMEM((entries, 2 * vectors, block), jnp.bfloat16),
            pltpu.VMEM((ITERS + 1, block_rows, vectors, block), jnp.float32),
            pltpu.VMEM((ITERS, shared, vectors, block), jnp.float32),
            pltpu.VMEM((ITERS, bits, shared, vectors, block), jnp.float32),
            pltpu.VMEM((size_y, vectors // 2, 2 * vectors), jnp.float32),
            pltpu.VMEM((size_x, vectors // 2, 2 * vectors), jnp.float32),
            dma((block_rows,)),
            dma((ITERS, bits)),
            dma((ITERS, bits)),
            dma((max(size_y - 1, 1),)),
            dma((max(size_y - 1, 1),)),
            dma((max(size_x - 1, 1),)),
            dma((max(size_x - 1, 1),)),
        ],
        compiler_params=pltpu.CompilerParams(
            collective_id=0, has_side_effects=True, vmem_limit_bytes=63 * 1024 * 1024
        ),
    )(cols, boundary, tiles, current.T, previous.T)
    return filtered.T, gram


def solution(mesh):
    in_specs = (
        P(("gx", "gy"), None, None, None),
        P(("gx", "gy"), None),
        P(("gx", "gy"), None),
        P(("gx", "gy"), None),
        P(("gx", "gy"), None),
    )
    out_specs = (P(("gx", "gy"), None), P())
    return jax.shard_map(shards, mesh=mesh, in_specs=in_specs, out_specs=out_specs, check_vma=False)
```

time: 97.2 us -> 34.4 us (0.35)
  blocking collectives: 38.2 us -> 0 us
  Pallas kernels: 0 us -> 30.5 us
  starting transfers between devices: 17.5 us -> 0 us
  matrix products: 14.6 us -> 0 us
  local copies, waits for them, and re-layouts: 13.2 us -> 3.05 us
  waiting for transfers between devices: 6.51 us -> 0 us
  other arithmetic: 5.71 us -> 0 us
    psum x1 -> x0, blocking collectives: 38.2 us -> none  [shards(): gram = lax.psum(partial_gram, ('gx', 'gy')) / float(total_rows)]
    pallas_call x0 -> x1, Pallas kernels: none -> 30.5 us  [shards(): pl.pallas_call(functools.partial(kernel, size_x, size_y, rows * size_x *...]
    ppermute x15 -> x0, starting transfers between devices: 17.5 us -> none  [partner(): return lax.ppermute(value, axis, pairs)]
    dot_general x4 -> x0, matrix products: 14.6 us -> none  [the longest x3 14.3 us: shards(): jnp.einsum('rtij,rtjv->riv', tiles, operands, precision=lax.Precision.HIG...]
    gather x6 -> x0, local copies, waits for them, and re-layouts: 6.74 us -> none  [the longest x3 5.09 us: shards(): operands = jnp.take(table, cols, axis=0)]
    ppermute x15 -> x0, waiting for transfers between devices: 6.51 us -> none  [partner(): return lax.ppermute(value, axis, pairs)]
    unnamed x38 -> x2, local copies, waits for them, and re-layouts: 4.88 us -> 3.05 us
    select_n x5 -> x0, other arithmetic: 1.57 us -> none  [the longest x4 0.88 us: shards(): outgoing = jnp.take(blocks, boundary[0], axis=0)]
  transfers between devices with their start and end apart: 15 -> 0, of which waited for: 3 -> 0; matrix products, arithmetic and copies ran while one was open for 7% -> 0% of each run, Pallas kernels for 0% -> 0%
where the time goes in v1:
time: 34.4 us; the launch traced here: 34.2 us
  Pallas kernels  30.5 us (89%)
  local copies, waits for them, and re-layouts  3.05 us (9%)
  between operations  0.64 us (2%)
    pallas_call x1, Pallas kernels, shards(): pl.pallas_call(functools.partial(kernel, size_x, size_y, rows * size_x *...  30.5 us
    unnamed x2, local copies, waits for them, and re-layouts  3.05 us

profile of v1, /device:TPU:0, one launch (start us, length us, event | category | flops | bytes accessed | tf_op | source)
XLA Modules:
  0.0 34.2 jit_solution(15581216438500041467)
XLA Ops:
  0.6 30.5 %shard_map.68 = (f32[64,1024]{1,0:T(8,128)}, f32[64,64]{1,0:T(8,128)}) custom-call(s32[8,5]{1,0:T(8,128)} %cols.1, s32[1,2]{1,0:T(1,128)} %boundary.1, f32[8,5,128,128]{3,2,1,0:T(8,128)} %tiles.1, f32[64,1024]{1,0:T(8,128)} %bitcast.4, f32[64,1024]{1,0:T(8,128)} %bitcast.5), custom_call_target="tpu_custom_call" | custom-call | tf_op jit(solution)/shard_map/pallas_call | solution.py:191
  31.1 1.7 %copy.9 = f32[1024,64]{0,1:T(8,128)} copy(f32[1024,64]{0,1:T(8,128)} %bitcast.3) | data formatting | bytes 524288
  32.8 1.4 %copy.10 = f32[64,64]{1,0:T(8,128)} copy(f32[64,64]{1,0:T(8,128)} %get-tuple-element.9) | data formatting | bytes 32768

commit v2 on v1

v2 whole, which is shorter than its diff:
```python
import functools

import jax
import jax.numpy as jnp
from jax import lax
from jax.experimental import pallas as pl
from jax.experimental.pallas import tpu as pltpu
from jax.sharding import PartitionSpec as P

ITERS = 3
GROUPS = 2
STRIP = 8
MESH = pl.DeviceIdType.MESH


def contract(a, b):
    return lax.dot_general(a, b, (((1,), (1,)), ((), ())), preferred_element_type=jnp.float32)


def split(x):
    high = x.astype(jnp.bfloat16)
    return high, (x - high.astype(jnp.float32)).astype(jnp.bfloat16)


def kernel(
    size_x,
    size_y,
    paired,
    total_rows,
    cols_in,
    boundary_in,
    tiles,
    current,
    previous,
    filtered,
    gram,
    cols,
    boundary,
    now,
    before,
    raw,
    pairs,
    table,
    fields,
    outgoing,
    ghosts,
    mine,
    pieces,
    sums,
    whole,
    load_sem,
    send_sem,
    recv_sem,
    send_y,
    recv_y,
    send_x,
    recv_x,
    send_back,
    recv_back,
):
    block_rows, per_row, block, _ = raw.shape
    vectors = fields.shape[2]
    _, groups, shared, width, _ = outgoing.shape
    i = lax.axis_index("gx")
    j = lax.axis_index("gy")

    partners = []
    for axis, size, me in (("gy", size_y, j), ("gx", size_x, i)):
        for bit in range(size.bit_length() - 1):
            stride = 2**bit
            partners.append({axis: me + stride - 2 * stride * ((me // stride) % 2)})
    bits_low = size_y.bit_length() - 1
    order = list(reversed(range(bits_low))) + list(range(bits_low, len(partners)))
    peers_y = [(j + k) % size_y for k in range(1, size_y)]
    peers_x = [(i + k) % size_x for k in range(1, size_x)]
    if paired:
        buddy = {"gx": i + 1 - 2 * (i % 2), "gy": j}
        shifts = [(m, n) for m in range(size_x // 2) for n in range(size_y) if m or n]
        others = [{"gx": (i + 2 * m) % size_x, "gy": (j + n) % size_y} for m, n in shifts]
        greeted = others + [buddy]
    else:
        greeted = [{"gy": n} for n in peers_y] + [{"gx": n} for n in peers_x]

    barrier = pltpu.get_barrier_semaphore()
    for peer in greeted:
        pl.semaphore_signal(barrier, inc=1, device_id=peer, device_id_type=MESH)

    ends = [(boundary_in, boundary), (current, now), (cols_in, cols), (previous, before)]
    ends += [(tiles.at[r], raw.at[r]) for r in range(block_rows)]
    loads = [pltpu.make_async_copy(a, b, load_sem.at[n]) for n, (a, b) in enumerate(ends)]
    for load in loads:
        load.start()

    def exchange(step, g):
        copies = {}
        for b in order:
            copies[b] = pltpu.make_async_remote_copy(
                src_ref=outgoing.at[step, g],
                dst_ref=ghosts.at[step, g, b],
                send_sem=send_sem.at[step * groups + g, b],
                recv_sem=recv_sem.at[step * groups + g, b],
                device_id=partners[b],
                device_id_type=MESH,
            )
            copies[b].start()
        return copies

    def enter(entry, g, value):
        high, low = split(value)
        table[entry, 2 * g * width : (2 * g + 1) * width, :] = high
        table[entry, (2 * g + 1) * width : (2 * g + 2) * width, :] = low

    def advance(step, r, first, last):
        operand = jnp.concatenate(
            [table[cols[r, t], 2 * first * width : 2 * last * width, :] for t in range(per_row)], axis=1
        )
        parts = contract(operand, pairs[r])
        products = []
        for g in range(last - first):
            high = parts[2 * g * width : (2 * g + 1) * width]
            low = parts[(2 * g + 1) * width : (2 * g + 2) * width]
            products.append(high[:, :block] + (low[:, :block] + high[:, block:]))
        product = jnp.concatenate(products, axis=0)
        span = slice(first * width, last * width)
        return 2.0 / 0.75 * (product - 0.25 * fields[step + 1, r, span, :]) - fields[step, r, span, :]

    def part(g):
        return slice(g * width, (g + 1) * width)

    loads[0].wait()
    loads[1].wait()
    for r in range(block_rows):
        fields[1, r] = now[:, r * block : (r + 1) * block]
    for s in range(shared):
        for g in range(groups):
            outgoing[0, g, s] = fields[1, boundary[0, s], part(g), :]
    pl.semaphore_wait(barrier, len(greeted))
    flights = [exchange(0, g) for g in range(groups)]
    started = [copy for copies in flights for copy in copies.values()]

    for r in range(block_rows):
        for g in range(groups):
            enter(r, g, fields[1, r, part(g), :])
    loads[2].wait()
    loads[3].wait()
    for r in range(block_rows):
        fields[0, r] = before[:, r * block : (r + 1) * block]
    for r in range(block_rows):
        loads[4 + r].wait()
        for t in range(per_row):
            high, low = split(raw[r, t])
            pairs[r, :block, t * block : (t + 1) * block] = high
            pairs[r, block:, t * block : (t + 1) * block] = low

    for step in range(ITERS):
        for g in range(groups):
            for b in reversed(order):
                flights[g][b].wait_recv()
                for s in range(shared):
                    enter(block_rows + b * shared + s, g, ghosts[step, g, b, s])
            if step < ITERS - 1:
                for s in range(shared):
                    outgoing[step + 1, g, s] = advance(step, boundary[0, s], g, g + 1)
                flights[g] = exchange(step + 1, g)
                started += flights[g].values()
        if step < ITERS - 1:
            for r in range(block_rows):
                fields[step + 2, r] = advance(step, r, 0, groups)
            for r in range(block_rows):
                for g in range(groups):
                    enter(r, g, fields[step + 2, r, part(g), :])
        else:
            halves = []
            for r in range(block_rows):
                value = advance(step, r, 0, groups)
                filtered[:, r * block : (r + 1) * block] = value
                halves.append(jnp.concatenate(split(value), axis=0))
            rows = jnp.concatenate(halves, axis=1)
            parts = contract(rows, rows)
            total = parts[:vectors, :vectors] + (parts[vectors:, :vectors] + parts[:vectors, vectors:])

    half = vectors // 2

    def share(moves_of, send, recv):
        moves = []
        for k, (source, target, peer) in enumerate(moves_of):
            moves.append(
                pltpu.make_async_remote_copy(
                    src_ref=source,
                    dst_ref=target,
                    send_sem=send.at[k],
                    recv_sem=recv.at[k],
                    device_id=peer,
                    device_id_type=MESH,
                )
            )
            moves[-1].start()
        for move in moves:
            move.wait_recv()
        return moves

    def added(terms):
        result = terms[0]
        for k in range(1, terms.shape[0]):
            result = result + terms[k]
        return result

    if paired:
        side = i % 2
        pair = (i // 2) * size_y + j
        strips = half // STRIP
        row = lax.broadcasted_iota(jnp.int32, (half, half), 0)
        column = lax.broadcasted_iota(jnp.int32, (half, half), 1)
        corner = total[half:, half:]
        mixed = jnp.where(row <= column, total[:half, :half], corner)
        diagonal = jnp.sum(jnp.where(row == column, corner, 0.0), axis=0, keepdims=True)
        spare = mine.shape[2] - half

        def fold(value):
            return jnp.concatenate([value[n * STRIP : (n + 1) * STRIP] for n in range(strips)], axis=1)

        def unfold(value):
            return jnp.concatenate([value[:, n * half : (n + 1) * half] for n in range(strips)], axis=0)

        mine[0, :STRIP, :] = fold(total[:half, half:])
        mine[0, STRIP:, :] = jnp.zeros((1, half + spare), jnp.float32)
        mine[1, :STRIP, :] = fold(mixed)
        mine[1, STRIP:, :] = jnp.concatenate([diagonal, jnp.zeros((1, spare), jnp.float32)], axis=1)
        started += share([(mine.at[1 - side], pieces.at[0], buddy)], send_x, recv_x)
        sums[pair] = mine[side] + pieces[0]
        started += share([(sums.at[pair], sums.at[pair], peer) for peer in others], send_y, recv_y)
        whole[side] = added(sums) / float(total_rows)
        started += share([(whole.at[side], whole.at[side], buddy)], send_back, recv_back)
        right = unfold(whole[0, :STRIP, :])
        mixed = unfold(whole[1, :STRIP, :])
        flipped = mixed.T
        diagonal = whole[1, STRIP:, :half]
        gram[:half, :half] = jnp.where(row <= column, mixed, flipped)
        gram[:half, half:] = right
        gram[half:, :half] = right.T
        gram[half:, half:] = jnp.where(row > column, mixed, jnp.where(row < column, flipped, diagonal))
    else:
        total = jnp.concatenate([total[:half], total[half:]], axis=1)
        height = half // size_x
        for n in range(size_x):
            mine[n] = total[n * height : (n + 1) * height]
        pieces[i] = mine[i]
        started += share([(mine.at[n], pieces.at[i], {"gx": n}) for n in peers_x], send_x, recv_x)
        sums[j] = added(pieces)
        started += share([(sums.at[j], sums.at[j], {"gy": n}) for n in peers_y], send_y, recv_y)
        whole[i] = added(sums) / float(total_rows)
        started += share([(whole.at[i], whole.at[i], {"gx": n}) for n in peers_x], send_back, recv_back)
        for n in range(size_x):
            gram[n * height : (n + 1) * height, :] = whole[n][:, :vectors]
            gram[half + n * height : half + (n + 1) * height, :] = whole[n][:, vectors:]
    for copy in started:
        copy.wait_send()


def deliver(filtered_in, gram_in, filtered, gram, sems):
    moves = [
        pltpu.make_async_copy(filtered_in, filtered, sems.at[0]),
        pltpu.make_async_copy(gram_in, gram, sems.at[1]),
    ]
    for move in moves:
        move.start()
    for move in moves:
        move.wait()


def shards(tiles, cols, boundary, current, previous):
    size_x = lax.axis_size("gx")
    size_y = lax.axis_size("gy")
    block_rows, per_row, block, _ = tiles.shape
    rows, vectors = current.shape
    shared = boundary.shape[1]
    bits = (size_x * size_y).bit_length() - 1
    entries = block_rows + bits * shared
    width = vectors // GROUPS
    paired = size_x % 2 == 0 and size_x * size_y <= 64
    if paired:
        pairs = size_x // 2 * size_y
        piece = (STRIP + 1, vectors // 2 * (vectors // 2 // STRIP))
        counts = (2, 1, pairs, 2)
    else:
        piece = (vectors // 2 // size_x, 2 * vectors)
        counts = (size_x, size_x, size_y, size_x)
    vmem = pl.BlockSpec(memory_space=pltpu.VMEM)
    hbm = pl.BlockSpec(memory_space=pltpu.HBM)
    dma = pltpu.SemaphoreType.DMA
    filtered, gram = pl.pallas_call(
        functools.partial(kernel, size_x, size_y, paired, rows * size_x * size_y),
        out_shape=(
            pltpu.VMEM((vectors, rows), jnp.float32),
            pltpu.VMEM((vectors, vectors), jnp.float32),
        ),
        in_specs=[hbm] * 5,
        out_specs=(vmem, vmem),
        scratch_shapes=[
            pltpu.SMEM(cols.shape, jnp.int32),
            pltpu.SMEM(boundary.shape, jnp.int32),
            pltpu.VMEM((vectors, rows), jnp.float32),
            pltpu.VMEM((vectors, rows), jnp.float32),
            pltpu.VMEM(tiles.shape, jnp.float32),
            pltpu.VMEM((block_rows, 2 * block, per_row * block), jnp.bfloat16),
            pltpu.VMEM((entries, 2 * vectors, block), jnp.bfloat16),
            pltpu.VMEM((ITERS + 1, block_rows, vectors, block), jnp.float32),
            pltpu.VMEM((ITERS, GROUPS, shared, width, block), jnp.float32),
            pltpu.VMEM((ITERS, GROUPS, bits, shared, width, block), jnp.float32),
            *[pltpu.VMEM((count, *piece), jnp.float32) for count in counts],
            dma((4 + block_rows,)),
            dma((ITERS * GROUPS, bits)),
            dma((ITERS * GROUPS, bits)),
            *[dma((max(counts),)) for _ in range(6)],
        ],
        compiler_params=pltpu.CompilerParams(
            collective_id=0, has_side_effects=True, vmem_limit_bytes=63 * 1024 * 1024
        ),
    )(cols, boundary, tiles, current.T, previous.T)
    filtered, gram = pl.pallas_call(
        deliver,
        out_shape=(
            jax.ShapeDtypeStruct((vectors, rows), jnp.float32),
            jax.ShapeDtypeStruct((vectors, vectors), jnp.float32),
        ),
        in_specs=[vmem, vmem],
        out_specs=(hbm, hbm),
        scratch_shapes=[dma((2,))],
        compiler_params=pltpu.CompilerParams(vmem_limit_bytes=1024 * 1024),
    )(filtered, gram)
    return filtered.T, gram


def solution(mesh):
    in_specs = (
        P(("gx", "gy"), None, None, None),
        P(("gx", "gy"), None),
        P(("gx", "gy"), None),
        P(("gx", "gy"), None),
        P(("gx", "gy"), None),
    )
    out_specs = (P(("gx", "gy"), None), P())
    return jax.shard_map(shards, mesh=mesh, in_specs=in_specs, out_specs=out_specs, check_vma=False)
```

time: 34.4 us -> 29.5 us (0.86)
  local copies, waits for them, and re-layouts: 3.05 us -> 0 us
  Pallas kernels: 30.5 us -> 28.7 us
    unnamed x2 -> x0, local copies, waits for them, and re-layouts: 3.05 us -> none
    pallas_call x1 -> x2, Pallas kernels: 30.5 us -> 28.7 us  [the longest x1 28 us: shards(): pl.pallas_call(functools.partial(kernel, size_x, size_y, paired, rows * s...]
where the time goes in v2:
time: 29.5 us; the launch traced here: 29.4 us
  Pallas kernels  28.7 us (97%)
  between operations  0.64 us (2%)
    pallas_call x1, Pallas kernels, shards(): pl.pallas_call(functools.partial(kernel, size_x, size_y, paired, rows * s...  28 us
    pallas_call x1, Pallas kernels, shards(): pl.pallas_call(deliver, out_shape=(jax.ShapeDtypeStruct((vectors, rows),...  0.72 us

profile of v2, /device:TPU:0, one launch (start us, length us, event | category | flops | bytes accessed | tf_op | source)
XLA Modules:
  0.0 29.4 jit_solution(6872896898408707294)
XLA Ops:
  0.6 28.0 %shard_map.68 = (f32[64,1024]{1,0:T(8,128)S(1)}, f32[64,64]{1,0:T(8,128)S(1)}) custom-call(s32[8,5]{1,0:T(8,128)} %cols_in.1, s32[1,2]{1,0:T(1,128)} %boundary_in.1, f32[8,5,128,128]{3,2,1,0:T(8,128)} %tiles.1, f32[64,1024]{1,0:T(8,128)} %bitcast.3, f32[64,1024]{1,0:T(8,128)} %bitcast.4), custom_call_target="tpu_custom_call" | custom-call | tf_op jit(solution)/shard_map/pallas_call | solution.py:291
  28.6 0.7 %shard_map.69 = (f32[64,1024]{1,0:T(8,128)}, f32[64,64]{1,0:T(8,128)}) custom-call(f32[64,1024]{1,0:T(8,128)S(1)} %get-tuple-element.6.filtered_in, f32[64,64]{1,0:T(8,128)S(1)} %get-tuple-element.7.gram_in), custom_call_target="tpu_custom_call" | custom-call | tf_op jit(solution)/shard_map/pallas_call | solution.py:320

commit v3 on v2

--- a/solution.py
+++ b/solution.py
@@ -70,14 +70,14 @@
             stride = 2**bit
             partners.append({axis: me + stride - 2 * stride * ((me // stride) % 2)})
     bits_low = size_y.bit_length() - 1
-    order = list(reversed(range(bits_low))) + list(range(bits_low, len(partners)))
+    order = list(reversed(range(bits_low))) + list(reversed(range(bits_low, len(partners))))
     peers_y = [(j + k) % size_y for k in range(1, size_y)]
     peers_x = [(i + k) % size_x for k in range(1, size_x)]
     if paired:
         buddy = {"gx": i + 1 - 2 * (i % 2), "gy": j}
         shifts = [(m, n) for m in range(size_x // 2) for n in range(size_y) if m or n]
         others = [{"gx": (i + 2 * m) % size_x, "gy": (j + n) % size_y} for m, n in shifts]
-        greeted = others + [buddy]
+        greeted = partners
     else:
         greeted = [{"gy": n} for n in peers_y] + [{"gx": n} for n in peers_x]
 
@@ -277,7 +277,7 @@
     bits = (size_x * size_y).bit_length() - 1
     entries = block_rows + bits * shared
     width = vectors // GROUPS
-    paired = size_x % 2 == 0 and size_x * size_y <= 64
+    paired = size_x % 2 == 0 and bits <= ITERS + 2
     if paired:
         pairs = size_x // 2 * size_y
         piece = (STRIP + 1, vectors // 2 * (vectors // 2 // STRIP))

time: 29.5 us -> 28.5 us (0.966)
  Pallas kernels: 28.7 us -> 27.7 us
    pallas_call x1, Pallas kernels: 28 us -> 27 us  [shards(): pl.pallas_call(functools.partial(kernel, size_x, size_y, paired, rows * s...]
where the time goes in v3:
time: 28.5 us; the launch traced here: 28.3 us
  Pallas kernels  27.7 us (97%)
  between operations  0.64 us (2%)
    pallas_call x1, Pallas kernels, shards(): pl.pallas_call(functools.partial(kernel, size_x, size_y, paired, rows * s...  27 us
    pallas_call x1, Pallas kernels, shards(): pl.pallas_call(deliver, out_shape=(jax.ShapeDtypeStruct((vectors, rows),...  0.72 us

profile of v3, /device:TPU:0, one launch (start us, length us, event | category | flops | bytes accessed | tf_op | source)
XLA Modules:
  0.0 28.3 jit_solution(5751945079387400831)
XLA Ops:
  0.6 27.0 %shard_map.68 = (f32[64,1024]{1,0:T(8,128)S(1)}, f32[64,64]{1,0:T(8,128)S(1)}) custom-call(s32[8,5]{1,0:T(8,128)} %cols_in.1, s32[1,2]{1,0:T(1,128)} %boundary_in.1, f32[8,5,128,128]{3,2,1,0:T(8,128)} %tiles.1, f32[64,1024]{1,0:T(8,128)} %bitcast.3, f32[64,1024]{1,0:T(8,128)} %bitcast.4), custom_call_target="tpu_custom_call" | custom-call | tf_op jit(solution)/shard_map/pallas_call | solution.py:291
  27.6 0.7 %shard_map.69 = (f32[64,1024]{1,0:T(8,128)}, f32[64,64]{1,0:T(8,128)}) custom-call(f32[64,1024]{1,0:T(8,128)S(1)} %get-tuple-element.6.filtered_in, f32[64,64]{1,0:T(8,128)S(1)} %get-tuple-element.7.gram_in), custom_call_target="tpu_custom_call" | custom-call | tf_op jit(solution)/shard_map/pallas_call | solution.py:320

commit v4 on v3

--- a/solution.py
+++ b/solution.py
@@ -75,7 +75,7 @@
     peers_x = [(i + k) % size_x for k in range(1, size_x)]
     if paired:
         buddy = {"gx": i + 1 - 2 * (i % 2), "gy": j}
-        shifts = [(m, n) for m in range(size_x // 2) for n in range(size_y) if m or n]
+        shifts = [(m, n) for m in reversed(range(size_x // 2)) for n in reversed(range(size_y)) if m or n]
         others = [{"gx": (i + 2 * m) % size_x, "gy": (j + n) % size_y} for m, n in shifts]
         greeted = partners
     else:
@@ -152,6 +152,7 @@
             pairs[r, :block, t * block : (t + 1) * block] = high
             pairs[r, block:, t * block : (t + 1) * block] = low
 
+    last = []
     for step in range(ITERS):
         for g in range(groups):
             for b in reversed(order):
@@ -163,6 +164,8 @@
                     outgoing[step + 1, g, s] = advance(step, boundary[0, s], g, g + 1)
                 flights[g] = exchange(step + 1, g)
                 started += flights[g].values()
+            else:
+                last.append([advance(step, r, g, g + 1) for r in range(block_rows)])
         if step < ITERS - 1:
             for r in range(block_rows):
                 fields[step + 2, r] = advance(step, r, 0, groups)
@@ -172,7 +175,7 @@
         else:
             halves = []
             for r in range(block_rows):
-                value = advance(step, r, 0, groups)
+                value = jnp.concatenate([values[r] for values in last], axis=0)
                 filtered[:, r * block : (r + 1) * block] = value
                 halves.append(jnp.concatenate(split(value), axis=0))
             rows = jnp.concatenate(halves, axis=1)

time: 28.5 us -> 28.7 us (level)
  no operation moved by 1% of the time
where the time goes in v4:
time: 28.7 us; the launch traced here: 28.5 us
  Pallas kernels  27.9 us (97%)
  between operations  0.64 us (2%)
    pallas_call x1, Pallas kernels, shards(): pl.pallas_call(functools.partial(kernel, size_x, size_y, paired, rows * s...  27.2 us
    pallas_call x1, Pallas kernels, shards(): pl.pallas_call(deliver, out_shape=(jax.ShapeDtypeStruct((vectors, rows),...  0.72 us

profile of v4, /device:TPU:0, one launch (start us, length us, event | category | flops | bytes accessed | tf_op | source)
XLA Modules:
  0.0 28.5 jit_solution(2157316443198403393)
XLA Ops:
  0.6 27.2 %shard_map.68 = (f32[64,1024]{1,0:T(8,128)S(1)}, f32[64,64]{1,0:T(8,128)S(1)}) custom-call(s32[8,5]{1,0:T(8,128)} %cols_in.1, s32[1,2]{1,0:T(1,128)} %boundary_in.1, f32[8,5,128,128]{3,2,1,0:T(8,128)} %tiles.1, f32[64,1024]{1,0:T(8,128)} %bitcast.3, f32[64,1024]{1,0:T(8,128)} %bitcast.4), custom_call_target="tpu_custom_call" | custom-call | tf_op jit(solution)/shard_map/pallas_call | solution.py:294
  27.8 0.7 %shard_map.69 = (f32[64,1024]{1,0:T(8,128)}, f32[64,64]{1,0:T(8,128)}) custom-call(f32[64,1024]{1,0:T(8,128)S(1)} %get-tuple-element.6.filtered_in, f32[64,64]{1,0:T(8,128)S(1)} %get-tuple-element.7.gram_in), custom_call_target="tpu_custom_call" | custom-call | tf_op jit(solution)/shard_map/pallas_call | solution.py:323
